TPU v7x, 32 devices: a whole 2x2x4 slice. The times are simulated.
32 devices in a mesh: ty: 8 (over z, x), tx: 4 (over y, core).
Axes of the slice: x: 2, y: 2, z: 4, core: 2. Of those that a mesh axis runs over, the one named last changes fastest.
Arguments:
- specimen: float32 [2, 2048, 4096], P(None, 'ty', 'tx'), may hold values from -5 to 5
- probe_modes: float32 [4, 2, 128, 128], replicated, may hold values from -0.75 to 0.75
- patterns: float32 [256, 128, 128], P(('ty', 'tx')), may hold values from 0.25 to 2.5
- tile_row: int32 [256], P(('ty', 'tx')), may hold values from 0 to 7, as said below
- row_offset: int32 [256], P(('ty', 'tx')), may hold values from 0 to 128
- col_offset: int32 [256], P(('ty', 'tx')), may hold values from 0 to 896
Outputs:
- specimen_out: float32 [2, 2048, 4096], P(None, 'ty', 'tx')
- probe_out: float32 [4, 2, 128, 128], replicated
Inputs may be any that keep to these rules, and one draw needn't show every extreme that they name: `tile_row`: each index of ty+tx holds 8 consecutive positions. At most 2 of one device's positions name the same tile row, and for every index of tx some tile row is named exactly 2 times by each device with that tx index.
All inputs are finite; a program needn't handle non-finite values.
Results may differ from a plain program's by a relative error of at most 0.0001.
Values sent between devices are 32-bit elements; how exact they have to be, the bound alone decides.
A program may use at most 192 MiB of HBM per device.

v0:
```python
import math

import jax
import jax.numpy as jnp
from jax import lax
from jax.sharding import PartitionSpec as P

ITERS = 2


AMP_FLOOR = 0.3
OBJ_STEP = 1.0
SMALL_EPS = 1e-06
HIGHEST_PREC = lax.Precision.HIGHEST


def dft_tables(length):
    counter = jnp.arange(length, dtype=jnp.int32)
    product = counter[:, None] * counter[None, :] % length
    angles = product.astype(jnp.float32) * (2.0 * math.pi / length)
    norming = 1.0 / math.sqrt(length)
    return (jnp.cos(angles) * norming, jnp.sin(angles) * norming)


def left_apply(matrix, values):
    return jnp.einsum("kn,abnx->abkx", matrix, values, precision=HIGHEST_PREC)


def right_apply(values, matrix):
    return jnp.einsum("abxn,nl->abxl", values, matrix, precision=HIGHEST_PREC)


def transform(real_part, imag_part, cos_table, sin_table, direction):
    real_mid = left_apply(cos_table, real_part) - direction * left_apply(sin_table, imag_part)
    imag_mid = left_apply(cos_table, imag_part) + direction * left_apply(sin_table, real_part)
    real_out = right_apply(real_mid, cos_table) - direction * right_apply(imag_mid, sin_table)
    imag_out = right_apply(imag_mid, cos_table) + direction * right_apply(real_mid, sin_table)
    return (real_out, imag_out)


def position_terms(windows, probe_modes, intensity, weight, cos_table, sin_table):
    spec_real = windows[:, 0][:, None]
    spec_imag = windows[:, 1][:, None]
    mode_real = probe_modes[:, 0][None]
    mode_imag = probe_modes[:, 1][None]
    wave_real = mode_real * spec_real - mode_imag * spec_imag
    wave_imag = mode_real * spec_imag + mode_imag * spec_real
    far_real, far_imag = transform(wave_real, wave_imag, cos_table, sin_table, -1.0)
    model_power = jnp.sum(far_real * far_real + far_imag * far_imag, axis=1)
    factor = jnp.sqrt(intensity) / jnp.maximum(jnp.sqrt(model_power), AMP_FLOOR) - 1.0
    back_real, back_imag = transform(
        far_real * factor[:, None], far_imag * factor[:, None], cos_table, sin_table, 1.0
    )
    grad_real = jnp.sum(mode_real * back_real + mode_imag * back_imag, axis=1)
    grad_imag = jnp.sum(mode_real * back_imag - mode_imag * back_real, axis=1)
    weights = weight[:, None, None, None]
    modes_real = jnp.sum(weights * (spec_real * back_real + spec_imag * back_imag), axis=0)
    modes_imag = jnp.sum(weights * (spec_real * back_imag - spec_imag * back_real), axis=0)
    grad_window = jnp.stack([grad_real, grad_imag], axis=1) * weights
    grad_modes = jnp.stack([modes_real, modes_imag], axis=1)
    lighting = jnp.sum(weight[:, None, None] * (windows[:, 0] ** 2 + windows[:, 1] ** 2), axis=0)
    return (grad_window, grad_modes, lighting)


def cut_windows(tile_field, rows_at, cols_at, window):
    anchor = jnp.int32(0)

    def cut_one(row_at, col_at):
        return lax.dynamic_slice(tile_field, (anchor, row_at, col_at), (2, window, window))

    return jax.vmap(cut_one)(rows_at, cols_at)


def deposit_windows(tile_field, updates, rows_at, cols_at):
    anchor = jnp.int32(0)
    window = updates.shape[-1]

    def deposit(position, running_field):
        corner = (anchor, rows_at[position], cols_at[position])
        region = lax.dynamic_slice(running_field, corner, (2, window, window))
        return lax.dynamic_update_slice(running_field, region + updates[position], corner)

    return lax.fori_loop(0, updates.shape[0], deposit, tile_field)


def shards(specimen, probe_modes, patterns, tile_row, row_offset, col_offset):
    own_count = patterns.shape[0]
    window = patterns.shape[-1]
    grid_rows = lax.axis_size("ty")
    capacity = max(2, 2 * own_count // grid_rows)
    slots_all = grid_rows * capacity
    cos_table, sin_table = dft_tables(window)
    serial = jnp.arange(own_count, dtype=jnp.int32)
    same_row = tile_row[:, None] == tile_row[None, :]
    earlier = serial[None, :] < serial[:, None]
    rank_in_row = jnp.sum(jnp.logical_and(same_row, earlier), axis=1)
    slot_of = tile_row * capacity + rank_in_row
    request_rows = jnp.stack([row_offset, col_offset, jnp.ones_like(row_offset)], axis=1)
    requests = jnp.zeros((slots_all, 3), jnp.int32).at[slot_of].set(request_rows)
    request_grid = requests.reshape(grid_rows, capacity, 3)
    pattern_grid = jnp.zeros((slots_all, window, window), jnp.float32).at[slot_of].set(patterns)
    pattern_grid = pattern_grid.reshape(grid_rows, capacity, window, window)
    seen_grid, measured = (
        lax.all_to_all(request_grid, "ty", split_axis=0, concat_axis=0, tiled=True),
        lax.all_to_all(pattern_grid, "ty", split_axis=0, concat_axis=0, tiled=True),
    )
    seen_flat = seen_grid.reshape(slots_all, 3)
    measured = measured.reshape(slots_all, window, window)
    valid = seen_flat[:, 2].astype(jnp.float32)
    for sweep_index in range(ITERS):
        probe_power = jnp.sum(probe_modes[:, 0] ** 2 + probe_modes[:, 1] ** 2, axis=0)
        obj_scale = OBJ_STEP / (jnp.max(probe_power) + SMALL_EPS)
        windows = cut_windows(specimen, seen_flat[:, 0], seen_flat[:, 1], window)
        grad_window, grad_modes, lighting = position_terms(
            windows, probe_modes, measured, valid, cos_table, sin_table
        )
        specimen = deposit_windows(
            specimen, obj_scale * grad_window, seen_flat[:, 0], seen_flat[:, 1]
        )
        grad_total, light_total = lax.psum((grad_modes, lighting), ("ty", "tx"))
        probe_modes = probe_modes + grad_total / (jnp.max(light_total) + SMALL_EPS)
    return (specimen, probe_modes)


def solution(mesh):
    placed = (
        P(None, "ty", "tx"),
        P(),
        P(("ty", "tx"), None, None),
        P(("ty", "tx")),
        P(("ty", "tx")),
        P(("ty", "tx")),
    )
    return jax.shard_map(
        shards, mesh=mesh, in_specs=placed, out_specs=(P(None, "ty", "tx"), P()), check_vma=False
    )
```

profile of v0, /device:TPU:0, one launch (start us, length us, event | category | flops | bytes accessed | tf_op | source)
XLA Modules:
  0.0 805.3 jit_solution(782398883551330315)
XLA Ops:
  9.5 7.3 all-to-all-start
  28.4 42.8 %while.30 = (s32[]{:T(128)}, f32[2,256,1024]{2,1,0:T(8,128)S(1)}, s32[16,3]{0,1:T(4,128)S(1)}, f32[16,2,128,128]{3,2,0,1:T(8,128)}, s32[]{:T(128)}) while((s32[]{:T(128)}, f32[2,256,1024]{2,1,0:T(8,128)S(1)}, s32[16,3]{0,1:T(4,128)S(1)}, f32[16,2,128,128]{3,2,0,1:T(8,128)}, s32[]{:T(128)}) %tuple.120), condition=%wide.while_cond, body=%wide.while_body.sunk | while | flops 2 | bytes 263785 | solution.py:69
  74.2 7.3 fusion.36
  81.5 7.4 multiply_add_fusion.6
  88.9 8.7 %fusion.26 = f32[16,4,128,128]{3,2,1,0:T(8,128)} fusion(f32[16,4,128,128]{3,2,1,0:T(8,128)S(1)} %multiply_add_fusion.6), kind=kOutput, calls=%fused_computation.34 | convolution fusion | flops 1610858496 | bytes 8388608 | tf_op jit(solution)/shard_map/abxn,nl->abxl/dot_general | solution.py:30
  97.6 8.7 %fusion.24 = f32[16,4,128,128]{3,2,1,0:T(8,128)} fusion(f32[16,4,128,128]{3,2,1,0:T(8,128)S(1)} %multiply_add_fusion.6), kind=kOutput, calls=%fused_computation.32 | convolution fusion | flops 1610858496 | bytes 8388608 | tf_op jit(solution)/shard_map/abxn,nl->abxl/dot_general | solution.py:30
  106.3 9.0 %fusion.37 = f32[16,4,128,128]{3,2,1,0:T(8,128)} fusion(f32[16,128,128]{2,1,0:T(8,128)S(1)} %get-tuple-element.267, f32[4,128,128]{2,1,0:T(8,128)S(1)} %get-tuple-element.271, f32[16,128,128]{2,1,0:T(8,128)S(1)} %get-tuple-element.266, f32[4,128,128]{2,1,0:T(8,128)S(1)} %get-tuple-element.270), kind=kOutput, calls=%fused_computation.66 | convolution fusion | flops 1614004224 | bytes 6815744 | tf_op jit(solution)/shard_map/kn,abnx->abkx/dot_general | solution.py:26
  115.4 9.4 %multiply_subtract_fusion.6 = f32[16,4,128,128]{3,2,1,0:T(8,128)S(1)} fusion(f32[16,4,128,128]{3,2,1,0:T(8,128)} %fusion.37, f32[16,128,128]{2,1,0:T(8,128)S(1)} %get-tuple-element.267, f32[4,128,128]{2,1,0:T(8,128)S(1)} %get-tuple-element.271, f32[16,128,128]{2,1,0:T(8,128)S(1)} %get-tuple-element.266, f32[4,128,128]{2,1,0:T(8,128)S(1)} %get-tuple-element.270), kind=kOutput, calls=%fused_computation.63 | convolution fusion | flops 1616101376 | bytes 11010048 | tf_op jit(solution)/shard_map/kn,abnx->abkx/dot_general | solution.py:26
  133.7 10.3 %add_reduce_fusion.3 = (f32[16,128,128]{2,1,0:T(8,128)}, f32[16,4,128,128]{3,2,1,0:T(8,128)}) fusion(f32[16,4,128,128]{3,2,1,0:T(8,128)S(1)} %multiply_subtract_fusion.5, f32[16,4,128,128]{3,2,1,0:T(8,128)S(1)} %copy-done.4, f32[16,4,128,128]{3,2,1,0:T(8,128)S(1)} %multiply_subtract_fusion.6), kind=kOutput, calls=%fused_computation.59 | convolution fusion | flops 1616887808 | bytes 17825792 | tf_op jit(solution)/shard_map/abxn,nl->abxl/dot_general | solution.py:30
  197.3 11.2 %multiply_reduce_fusion.3 = (f32[4,128,128]{2,1,0:T(8,128)}, f32[4,128,128]{2,1,0:T(8,128)}, f32[16,128,128]{2,1,0:T(8,128)S(1)}, f32[16,128,128]{2,1,0:T(8,128)S(1)}) fusion(f32[16,4,128,128]{3,2,1,0:T(8,128)S(1)} %fusion.60, f32[16]{0:T(128)S(1)} %bitcast.253, f32[16,128,128]{2,1,0:T(8,128)S(1)} %get-tuple-element.267, ...), kind=kOutput, calls=%fused_computation.56 | convolution fusion | flops 1630126080 | bytes 17825856 | tf_op jit(solution)/shard_map/abxn,nl->abxl/dot_general | solution.py:30
  210.9 134.5 %while.28 = (s32[]{:T(128)}, f32[2,256,1024]{2,1,0:T(8,128)S(1)}, s32[16]{0:T(128)S(1)}, s32[16]{0:T(128)S(1)}, f32[16,2,128,128]{3,2,1,0:T(8,128)}, /*index=5*/s32[]{:T(128)}, s32[]{:T(128)}, s32[]{:T(128)}, s32[]{:T(128)}) while((s32[]{:T(128)}, f32[2,256,1024]{2,1,0:T(8,128)S(1)}, s32[16]{0:T(128)S(1)}, s32[16]{0:T(128)S(1)}, ...), condition=%wide.region_9.10_spmd, body=%wide.region_8.9_spmd.sunk | while | flops 32776 | bytes 655561 | solution.py:83
  345.4 42.9 %while.31 = (s32[]{:T(128)}, f32[2,256,1024]{2,1,0:T(8,128)S(1)}, s32[16,3]{0,1:T(4,128)S(1)}, f32[16,2,128,128]{3,2,1,0:T(8,128)}, s32[]{:T(128)}) while((s32[]{:T(128)}, f32[2,256,1024]{2,1,0:T(8,128)S(1)}, s32[16,3]{0,1:T(4,128)S(1)}, f32[16,2,128,128]{3,2,1,0:T(8,128)}, s32[]{:T(128)}) %tuple.121), condition=%wide.while_cond.1, body=%wide.while_body.1.sunk | while | flops 2 | bytes 263785 | solution.py:69
  396.1 127.7 %all-reduce.7.cloned.1.call-done = (f32[4,2,128,128]{3,2,1,0:T(8,128)}, f32[128,128]{1,0:T(8,128)}) async-done(((f32[4,2,128,128]{3,2,1,0:T(8,128)}, f32[128,128]{1,0:T(8,128)}), (f32[4,2,128,128]{3,2,1,0:T(8,128)}, f32[128,128]{1,0:T(8,128)})) %all-reduce.7.cloned.1.call-update) | async-done | bytes 589840 | tf_op jit(solution)/shard_map/psum | solution.py:120
  534.4 7.6 fusion.32
  549.2 7.5 fusion.10
  563.9 7.4 multiply_subtract_fusion.1
  586.0 7.6 fusion.42
  600.7 7.4 fusion.85
  608.1 9.5 %fusion.2 = f32[16,4,128,128]{3,2,1,0:T(8,128)} fusion(f32[16,4,128,128]{3,2,1,0:T(8,128)S(1)} %fusion.85), kind=kOutput, calls=%fused_computation.10 | convolution fusion | flops 1610858496 | bytes 8388608 | tf_op jit(solution)/shard_map/abxn,nl->abxl/dot_general | solution.py:30
  617.6 8.6 %fusion = f32[16,4,128,128]{3,2,1,0:T(8,128)} fusion(f32[16,4,128,128]{3,2,1,0:T(8,128)S(1)} %fusion.85), kind=kOutput, calls=%fused_computation.8 | convolution fusion | flops 1610858496 | bytes 8388608 | tf_op jit(solution)/shard_map/abxn,nl->abxl/dot_general | solution.py:30
  626.3 8.6 %fusion.82 = f32[16,4,128,128]{3,2,1,0:T(8,128)} fusion(f32[16,4,128,128]{3,2,1,0:T(8,128)S(1)} %fusion.42, f32[16,4,128,128]{3,2,1,0:T(8,128)S(1)} %multiply_subtract_fusion, f32[16,128,128]{2,1,0:T(8,128)S(1)} %fusion.131), kind=kOutput, calls=%fused_computation.92 | convolution fusion | flops 1612955648 | bytes 13631488 | tf_op jit(solution)/shard_map/kn,abnx->abkx/dot_general | solution.py:26
  636.2 10.0 %fusion.70 = f32[16,4,128,128]{3,2,1,0:T(8,128)S(1)} fusion(f32[16,4,128,128]{3,2,1,0:T(8,128)} %fusion.2, f32[16,4,128,128]{3,2,1,0:T(8,128)} %fusion.82), kind=kOutput, calls=%fused_computation.88 | convolution fusion | flops 1611907072 | bytes 12582912 | tf_op jit(solution)/shard_map/abxn,nl->abxl/dot_general | solution.py:30
  646.3 11.7 %multiply_reduce_fusion.1 = (f32[4,128,128]{2,1,0:T(8,128)S(1)}, f32[4,128,128]{2,1,0:T(8,128)S(1)}, f32[16,128,128]{2,1,0:T(8,128)}, f32[16,128,128]{2,1,0:T(8,128)}) fusion(f32[16,4,128,128]{3,2,1,0:T(8,128)S(1)} %fusion.70, f32[16,128,128]{2,1,0:T(8,128)S(1)} %slice_bitcast_fusion, f32[16,128,128]{2,1,0:T(8,128)S(1)} %slice_bitcast_fusion.1, ...), kind=kOutput, calls=%fused_computation.41 | convolution fusion | flops 1630126080 | bytes 17825856 | tf_op jit(solution)/shard_map/abxn,nl->abxl/dot_general | solution.py:30
  662.1 131.8 %while.29 = (s32[]{:T(128)}, f32[2,256,1024]{2,1,0:T(8,128)S(1)}, s32[16]{0:T(128)S(1)}, s32[16]{0:T(128)S(1)}, f32[16,2,128,128]{3,2,1,0:T(8,128)}, /*index=5*/s32[]{:T(128)}, s32[]{:T(128)}, s32[]{:T(128)}, s32[]{:T(128)}) while((s32[]{:T(128)}, f32[2,256,1024]{2,1,0:T(8,128)S(1)}, s32[16]{0:T(128)S(1)}, s32[16]{0:T(128)S(1)}, ...), condition=%wide.region_22.23_spmd, body=%wide.region_21.22_spmd.sunk | while | flops 32776 | bytes 655561 | solution.py:83
  (334 shorter events, 373.2 us)
Async XLA Ops:
  7.2 9.6 %copy-start.18 = (f32[4,2,128,128]{3,2,1,0:T(8,128)S(1)}, f32[4,2,128,128]{3,2,1,0:T(8,128)}, u32[]{:S(2)}) copy-start(f32[4,2,128,128]{3,2,1,0:T(8,128)} %param.11) | copy-start | bytes 1572868
  7.9 20.5 %copy-start.11 = (f32[2,256,1024]{2,1,0:T(8,128)S(1)}, f32[2,256,1024]{2,1,0:T(8,128)}, u32[]{:S(2)}) copy-start(f32[2,256,1024]{2,1,0:T(8,128)} %param.10) | copy-start | bytes 6291460
  9.5 13.8 %all-to-all-start = ((s32[8,2,3]{2,1,0:T(2,128)}), s32[8,2,3]{2,1,0:T(2,128)S(1)}, u32[]{:S(2)}, u32[]{:S(2)}) async-start(s32[8,2,3]{2,1,0:T(2,128)} %bitcast.8), calls=%async_computation | async-start | bytes 16384 | tf_op jit(solution)/shard_map/all_to_all | solution.py:104
  16.8 98.5 %copy-start.14 = (f32[4,128,128]{2,1,0:T(8,128)}, f32[4,128,128]{2,1,0:T(8,128)S(1)}, u32[]{:S(2)}) copy-start(f32[4,128,128]{2,1,0:T(8,128)S(1)} %get-tuple-element.271) | copy-start | bytes 786436
  23.3 120.7 %all-to-all-start.1 = ((f32[8,2,128,128]{3,2,1,0:T(8,128)}), f32[8,2,128,128]{3,2,1,0:T(8,128)}, u32[]{:S(2)}, u32[]{:S(2)}) async-start(f32[8,2,128,128]{3,2,1,0:T(8,128)} %bitcast.24), calls=%async_computation.1 | async-start | bytes 2097152 | tf_op jit(solution)/shard_map/all_to_all | solution.py:105
  28.1 495.7 %all-reduce.7.cloned.1.call-start = ((), (), s32[]{:S(2)}) async-start(), calls=%async_computation.3 | async-start | bytes 1179648 | tf_op jit(solution)/shard_map/psum | solution.py:120
  115.4 9.4 %copy-start.5 = (f32[16,4,128,128]{3,2,1,0:T(8,128)S(1)}, f32[16,4,128,128]{3,2,1,0:T(8,128)}, u32[]{:S(2)}) copy-start(f32[16,4,128,128]{3,2,1,0:T(8,128)} %fusion.26) | copy-start | bytes 12582916
  124.8 8.9 %copy-start.4 = (f32[16,4,128,128]{3,2,1,0:T(8,128)S(1)}, f32[16,4,128,128]{3,2,1,0:T(8,128)}, u32[]{:S(2)}) copy-start(f32[16,4,128,128]{3,2,1,0:T(8,128)} %fusion.24) | copy-start | bytes 12582916
  144.0 3.3 copy-start.2
  154.2 7.3 copy-start.1
  190.0 7.3 copy-start.15
  208.5 2.3 copy-start.7
  210.9 181.5 %copy-start.20 = (f32[4,128,128]{2,1,0:T(8,128)S(1)}, f32[4,128,128]{2,1,0:T(8,128)}, u32[]{:S(2)}) copy-start(f32[4,128,128]{2,1,0:T(8,128)} %get-tuple-element.210) | copy-start | bytes 786436
  388.3 5.0 copy-start.8
  388.3 4.1 copy-start.21
  393.2 400.7 %all-reduce.5.cloned.1.call-start = ((), (), s32[]{:S(2)}) async-start(), calls=%async_computation.2 | async-start | bytes 1179648 | tf_op jit(solution)/shard_map/psum | solution.py:120
  527.1 99.1 %copy-start.12 = (f32[4,2,128,128]{3,2,1,0:T(8,128)}, f32[4,2,128,128]{3,2,1,0:T(8,128)S(1)}, u32[]{:S(2)}) copy-start(f32[4,2,128,128]{3,2,1,0:T(8,128)S(1)} %divide_add_fusion.1) | copy-start | bytes 1572868
  527.2 36.7 %copy-start.16 = (f32[4,128,128]{2,1,0:T(8,128)}, f32[4,128,128]{2,1,0:T(8,128)S(1)}, u32[]{:S(2)}) copy-start(f32[4,128,128]{2,1,0:T(8,128)S(1)} %get-tuple-element.269) | copy-start | bytes 786436
  636.2 10.1 %copy-start.3 = (f32[16,4,128,128]{3,2,1,0:T(8,128)S(1)}, f32[16,4,128,128]{3,2,1,0:T(8,128)}, u32[]{:S(2)}) copy-start(f32[16,4,128,128]{3,2,1,0:T(8,128)} %fusion.82) | copy-start | bytes 12582916
  636.2 10.1 %copy-start.17 = (f32[4,128,128]{2,1,0:T(8,128)S(1)}, f32[4,128,128]{2,1,0:T(8,128)}, u32[]{:S(2)}) copy-start(f32[4,128,128]{2,1,0:T(8,128)} %copy-done.16) | copy-start | bytes 786436
  636.2 10.1 %copy-start.19 = (f32[16,4,128,128]{3,2,1,0:T(8,128)S(1)}, f32[16,4,128,128]{3,2,1,0:T(8,128)}, u32[]{:S(2)}) copy-start(f32[16,4,128,128]{3,2,1,0:T(8,128)} %fusion) | copy-start | bytes 12582916
  658.0 4.2 copy-start.9
  658.8 137.3 %copy-start.13 = (f32[4,2,128,128]{3,2,1,0:T(8,128)S(1)}, f32[4,2,128,128]{3,2,1,0:T(8,128)}, u32[]{:S(2)}) copy-start(f32[4,2,128,128]{3,2,1,0:T(8,128)} %copy-done.12) | copy-start | bytes 1572868
  793.9 4.1 copy-start.10
  (5 other events, 5.9 us)
Sparse Core Ops, SparseCore 0:
  393.4 130.3 all-reduce.6
  658.9 129.2 all-reduce.4
where the time goes:
time: 818 us; the launch traced here: 805 us
  matrix products  258 us (32%)
  local copies, waits for them, and re-layouts  214 us (26%)
  waiting for transfers between devices  129 us (16%)
  loops' own time  122 us (15%)
  other arithmetic  53.2 us (7%)
  between operations  17.6 us (2%)
  starting transfers between devices  12.3 us (2%)
    dot_general x16, matrix products, right_apply(): return jnp.einsum('abxn,nl->abxl', values, matrix, precision=HIGHEST_PREC)  136 us
    psum x2, waiting for transfers between devices, shards(): grad_total, light_total = lax.psum((grad_modes, lighting), ('ty', 'tx'))  128 us
    another operation x2, loops' own time, deposit_windows(): return lax.fori_loop(0, updates.shape[0], deposit, tile_field)  122 us
    dot_general x16, matrix products, left_apply(): return jnp.einsum('kn,abnx->abkx', matrix, values, precision=HIGHEST_PREC)  121 us
    gather x96, local copies, waits for them, and re-layouts  85.6 us
    dynamic_update_slice x32, local copies, waits for them, and re-layouts, deposit(): lax.dynamic_update_slice(running_field, region + updates[position], corner)  72.2 us
    dynamic_slice x64, local copies, waits for them, and re-layouts, deposit(): corner = (anchor, rows_at[position], cols_at[position])  40 us
    add x32, other arithmetic, deposit(): region + updates[position]  32.6 us
  transfers between devices with their start and end apart: 4, of which 2 were waited for; matrix products, arithmetic and copies ran while one was open for 24% of the time, Pallas kernels for 0%

commit v1 on v0

v1 whole, which is shorter than its diff:
```python
import functools
import math

import jax
import jax.numpy as jnp
import ml_dtypes
import numpy as np
from jax import lax
from jax.experimental import pallas as pl
from jax.experimental.pallas import tpu as pltpu
from jax.sharding import PartitionSpec as P

ITERS = 2
AMP_FLOOR = 0.3
OBJ_STEP = 1.0
SMALL_EPS = 1e-06

VMEM = pltpu.VMEM
SMEM = pltpu.SMEM
LIMIT = 50 * 1024 * 1024


def dft_tables(length):
    counter = np.arange(length, dtype=np.int64)
    angles = (counter[:, None] * counter[None, :] % length) * (2.0 * math.pi / length)
    cos = np.cos(angles) / math.sqrt(length)
    sin = np.sin(angles) / math.sqrt(length)
    one = np.block([[cos, sin], [-sin, cos]])
    parts = []
    for table in (one, one.T):
        high = table.astype(ml_dtypes.bfloat16)
        low = (table - high.astype(np.float64)).astype(ml_dtypes.bfloat16)
        parts += [high, low]
    return np.stack(parts)


def split(values):
    high = values.astype(jnp.bfloat16)
    low = (values - high.astype(jnp.float32)).astype(jnp.bfloat16)
    return high, low


def dot(a, b):
    return jnp.dot(a, b, preferred_element_type=jnp.float32)


def left(high, low, values):
    v_high, v_low = split(values)
    return dot(high, v_high) + (dot(low, v_high) + dot(high, v_low))


def right(values, high, low):
    v_high, v_low = split(values)
    return dot(v_high, high) + (dot(v_low, high) + dot(v_high, low))


def bucket_kernel(capacity, tile_ref, row_ref, col_ref, patterns_ref, grid_ref, req_ref):
    own = patterns_ref.shape[0]

    def clear(j, carry):
        req_ref[j] = 0
        return carry

    lax.fori_loop(0, req_ref.shape[0], clear, 0)
    for p in range(own):
        tile = tile_ref[p]
        rank = jnp.int32(0)
        for q in range(p):
            rank = rank + (tile_ref[q] == tile).astype(jnp.int32)
        slot = tile * capacity + rank
        grid_ref[slot] = patterns_ref[p]
        req_ref[slot * 3] = row_ref[p]
        req_ref[slot * 3 + 1] = col_ref[p]
        req_ref[slot * 3 + 2] = jnp.int32(1)


def bucket(tile_row, row_offset, col_offset, patterns, slots, capacity):
    window = patterns.shape[-1]
    return pl.pallas_call(
        functools.partial(bucket_kernel, capacity),
        out_shape=(
            jax.ShapeDtypeStruct((slots, window, window), jnp.float32),
            jax.ShapeDtypeStruct((slots * 3,), jnp.int32),
        ),
        in_specs=[pl.BlockSpec(memory_space=SMEM)] * 3 + [pl.BlockSpec(memory_space=VMEM)],
        out_specs=(pl.BlockSpec(memory_space=VMEM), pl.BlockSpec(memory_space=SMEM)),
        name="bucket",
    )(tile_row, row_offset, col_offset, patterns)


def sweep_kernel(req_ref, spec_ref, probe_ref, table_ref, pattern_ref, out_ref, grad_ref, scale_ref, far_ref):
    step = pl.program_id(0)
    modes, _, window, _ = probe_ref.shape
    tiles = window // 8

    @pl.when(step == 0)
    def _():
        out_ref[...] = spec_ref[...]
        grad_ref[...] = jnp.zeros_like(grad_ref)
        power = jnp.zeros((window, window), jnp.float32)
        for m in range(modes):
            power = power + (probe_ref[m, 0] ** 2 + probe_ref[m, 1] ** 2)
        scale_ref[0] = OBJ_STEP / (jnp.max(power) + SMALL_EPS)

    @pl.when(req_ref[step * 3 + 2] > 0)
    def _():
        row = req_ref[step * 3]
        col = req_ref[step * 3 + 1]
        row0 = jnp.minimum(row // 8, spec_ref.shape[1] - tiles - 1)
        col0 = jnp.minimum(col // window, spec_ref.shape[3] // window - 2)
        row_s = row - row0 * 8
        col_s = col - col0 * window
        lanes = pl.multiple_of(col0 * window, window)
        lanes2 = pl.multiple_of(col0 * window + window, window)
        sub8 = lax.broadcasted_iota(jnp.int32, (tiles, 8, window), 1)
        lane17 = lax.broadcasted_iota(jnp.int32, (tiles + 1, 8, window), 2)
        col_back = lax.rem(window - col_s, window)
        row_back = lax.rem(8 - row_s, 8)
        cut = []
        for plane in range(2):
            first = spec_ref[plane, pl.ds(row0, tiles + 1), :, pl.ds(lanes, window)]
            second = spec_ref[plane, pl.ds(row0, tiles + 1), :, pl.ds(lanes2, window)]
            joined = jnp.where(
                lane17 < window - col_s,
                pltpu.roll(first, col_back, 2),
                pltpu.roll(second, col_back, 2),
            )
            turned = pltpu.roll(joined, row_back, 1)
            picked = jnp.where(sub8 < 8 - row_s, turned[:tiles], turned[1:])
            cut.append(picked.reshape(window, window))
        w_re, w_im = cut
        grad_ref[modes * 2] += w_re * w_re + w_im * w_im

        power = jnp.zeros((window, window), jnp.float32)
        for pair in range(0, modes, 2):
            top, low = [], []
            for m in (pair, pair + 1):
                p_re, p_im = probe_ref[m, 0], probe_ref[m, 1]
                top.append(p_re * w_re - p_im * w_im)
                low.append(p_re * w_im + p_im * w_re)
            wave = jnp.concatenate(
                [jnp.concatenate(top, axis=1), jnp.concatenate(low, axis=1)], axis=0
            )
            mid = left(table_ref[0], table_ref[1], wave)
            for k, m in enumerate((pair, pair + 1)):
                lane = slice(k * window, (k + 1) * window)
                side = jnp.concatenate([mid[:window, lane], mid[window:, lane]], axis=1)
                far = right(side, table_ref[2], table_ref[3])
                far_ref[m] = far
                power = power + (far[:, :window] ** 2 + far[:, window:] ** 2)
        factor = jnp.sqrt(pattern_ref[0]) / jnp.maximum(jnp.sqrt(power), AMP_FLOOR) - 1.0
        factor2 = jnp.concatenate([factor, factor], axis=1)
        g_re = jnp.zeros((window, window), jnp.float32)
        g_im = jnp.zeros((window, window), jnp.float32)
        for pair in range(0, modes, 2):
            top, low = [], []
            for m in (pair, pair + 1):
                side = right(far_ref[m] * factor2, table_ref[0], table_ref[1])
                top.append(side[:, :window])
                low.append(side[:, window:])
            mid = jnp.concatenate(
                [jnp.concatenate(top, axis=1), jnp.concatenate(low, axis=1)], axis=0
            )
            back = left(table_ref[2], table_ref[3], mid)
            for k, m in enumerate((pair, pair + 1)):
                lane = slice(k * window, (k + 1) * window)
                b_re, b_im = back[:window, lane], back[window:, lane]
                p_re, p_im = probe_ref[m, 0], probe_ref[m, 1]
                g_re = g_re + (p_re * b_re + p_im * b_im)
                g_im = g_im + (p_re * b_im - p_im * b_re)
                grad_ref[2 * m] += w_re * b_re + w_im * b_im
                grad_ref[2 * m + 1] += w_re * b_im - w_im * b_re

        scale = scale_ref[0]
        lane16 = lax.broadcasted_iota(jnp.int32, (tiles + 1, 8, window), 2)
        sub17 = lax.broadcasted_iota(jnp.int32, (tiles + 1, 8, window), 1)
        row_turn = lax.rem(row_s, 8)
        col_turn = lax.rem(col_s, window)
        none = jnp.zeros((1, 8, window), jnp.float32)
        for plane, grad in enumerate((g_re, g_im)):
            turned = pltpu.roll((grad * scale).reshape(tiles, 8, window), row_turn, 1)
            spread = jnp.where(
                sub17 >= row_s,
                jnp.concatenate([turned, none], axis=0),
                jnp.concatenate([none, turned], axis=0),
            )
            spread = pltpu.roll(spread, col_turn, 2)
            out_ref[plane, pl.ds(row0, tiles + 1), :, pl.ds(lanes, window)] += jnp.where(
                lane16 >= col_s, spread, 0.0
            )
            out_ref[plane, pl.ds(row0, tiles + 1), :, pl.ds(lanes2, window)] += jnp.where(
                lane16 < col_s, spread, 0.0
            )


def sweep(requests, specimen, probe_modes, tables, measured):
    slots, window, _ = measured.shape
    modes = probe_modes.shape[0]
    whole = lambda shape: pl.BlockSpec(shape, lambda i: (0,) * len(shape))
    return pl.pallas_call(
        sweep_kernel,
        grid=(slots,),
        out_shape=(
            jax.ShapeDtypeStruct(specimen.shape, jnp.float32),
            jax.ShapeDtypeStruct((2 * modes + 1, window, window), jnp.float32),
        ),
        in_specs=[
            pl.BlockSpec(memory_space=SMEM),
            whole(specimen.shape),
            whole(probe_modes.shape),
            whole(tables.shape),
            pl.BlockSpec((1, window, window), lambda i: (i, 0, 0)),
        ],
        out_specs=(whole(specimen.shape), whole((2 * modes + 1, window, window))),
        scratch_shapes=[
            pltpu.SMEM((1,), jnp.float32),
            pltpu.VMEM((modes, window, 2 * window), jnp.float32),
        ],
        compiler_params=pltpu.CompilerParams(
            dimension_semantics=("arbitrary",), vmem_limit_bytes=LIMIT
        ),
        name="sweep",
    )(requests, specimen, probe_modes, tables, measured)


def shards(specimen, probe_modes, patterns, tile_row, row_offset, col_offset):
    own_count = patterns.shape[0]
    window = patterns.shape[-1]
    modes = probe_modes.shape[0]
    grid_rows = lax.axis_size("ty")
    capacity = max(2, 2 * own_count // grid_rows)
    slots = grid_rows * capacity
    tables = jnp.asarray(dft_tables(window))
    pattern_grid, requests = bucket(tile_row, row_offset, col_offset, patterns, slots, capacity)
    seen = lax.all_to_all(
        requests.reshape(grid_rows, capacity * 3), "ty", split_axis=0, concat_axis=0, tiled=True
    ).reshape(slots * 3)
    measured = lax.all_to_all(
        pattern_grid.reshape(grid_rows, capacity, window, window),
        "ty", split_axis=0, concat_axis=0, tiled=True,
    ).reshape(slots, window, window)
    shape = specimen.shape
    specimen = specimen.reshape(2, shape[1] // 8, 8, shape[2])
    for sweep_index in range(ITERS):
        specimen, grads = sweep(seen, specimen, probe_modes, tables, measured)
        total = lax.psum(grads, ("ty", "tx"))
        probe_modes = probe_modes + total[: 2 * modes].reshape(probe_modes.shape) / (
            jnp.max(total[2 * modes]) + SMALL_EPS
        )
    return (specimen.reshape(shape), probe_modes)


def solution(mesh):
    placed = (
        P(None, "ty", "tx"),
        P(),
        P(("ty", "tx"), None, None),
        P(("ty", "tx")),
        P(("ty", "tx")),
        P(("ty", "tx")),
    )
    return jax.shard_map(
        shards, mesh=mesh, in_specs=placed, out_specs=(P(None, "ty", "tx"), P()), check_vma=False
    )
```

time: 818 us -> 392 us (0.48); the launches traced: 805 us -> 391 us
  matrix products: 258 us -> 0 us
  local copies, waits for them, and re-layouts: 214 us -> 1.34 us
  waiting for transfers between devices: 129 us -> 302 us
  loops' own time: 122 us -> 0 us
  Pallas kernels: 0 us -> 48.6 us
  other arithmetic: 53.2 us -> 6.7 us
  blocking collectives: 0 us -> 13.6 us
  starting transfers between devices: 12.3 us -> 3.64 us
    dot_general x32 -> x0, matrix products: 258 us -> none  [the longest x16 136 us: right_apply(): return jnp.einsum('abxn,nl->abxl', values, matrix, precision=HIGHEST_PREC)]
    psum x2, waiting for transfers between devices: 128 us -> 278 us  [shards(): total = lax.psum(grads, ('ty', 'tx'))]
    another operation x4 -> x0, loops' own time: 122 us -> none  [the longest x2 122 us: deposit_windows(): return lax.fori_loop(0, updates.shape[0], deposit, tile_field)]
    gather x96 -> x0, local copies, waits for them, and re-layouts: 85.6 us -> none
    dynamic_update_slice x32 -> x0, local copies, waits for them, and re-layouts: 72.2 us -> none  [deposit(): lax.dynamic_update_slice(running_field, region + updates[position], corner)]
    pallas_call x0 -> x3, Pallas kernels: none -> 48.6 us  [the longest x2 46.1 us: sweep(): pl.pallas_call(sweep_kernel, grid=(slots,), out_shape=(jax.ShapeDtypeStru...]
    dynamic_slice x64 -> x0, local copies, waits for them, and re-layouts: 40 us -> none  [deposit(): corner = (anchor, rows_at[position], cols_at[position])]
    add x34 -> x2, other arithmetic: 35.7 us -> 0.95 us  [shards(): probe_modes + total[:2 * modes].reshape(probe_modes.shape) / (jnp.max(tot...]
  transfers between devices with their start and end apart: 4 -> 3, of which waited for: 2 -> 3; matrix products, arithmetic and copies ran while one was open for 24% -> 0% of each run, Pallas kernels for 0% -> 0%
where the time goes in v1:
time: 392 us; the launch traced here: 391 us
  waiting for transfers between devices  302 us (77%)
  Pallas kernels  48.6 us (12%)
  between operations  15.4 us (4%)
  blocking collectives  13.6 us (3%)
  other arithmetic  6.7 us (2%)
    psum x2, waiting for transfers between devices, shards(): total = lax.psum(grads, ('ty', 'tx'))  278 us
    pallas_call x2, Pallas kernels, sweep(): pl.pallas_call(sweep_kernel, grid=(slots,), out_shape=(jax.ShapeDtypeStru...  46.1 us
    all_to_all x1, waiting for transfers between devices, shards(): lax.all_to_all(pattern_grid.reshape(grid_rows, capacity, window, window),...  23.4 us
    all_to_all x1, blocking collectives, shards(): lax.all_to_all(requests.reshape(grid_rows, capacity * 3), 'ty', split_axi...  13.6 us
  transfers between devices with their start and end apart: 3, of which 3 were waited for; matrix products, arithmetic and copies ran while one was open for 0% of the time, Pallas kernels for 0%

profile of v1, /device:TPU:0, one launch (start us, length us, event | category | flops | bytes accessed | tf_op | source)
XLA Modules:
  0.0 391.1 jit_solution(5944786033785213103)
XLA Ops:
  7.2 0.0 copy-start.1
  7.2 2.5 bucket.1
  9.7 0.7 all_to_all.9
  10.4 13.6 %all_to_all.14 = s32[8,1,6]{2,1,0:T(1,128)S(1)} all-to-all(s32[8,1,6]{2,1,0:T(1,128)S(1)} %bitcast.13), channel_id=1, replica_groups=mesh['ty'=8,'tx'=4] {'ty'}, dimensions={0} | all-to-all | bytes 384 | tf_op jit(solution)/shard_map/all_to_all | solution.py:235
  24.0 3.6 all-to-all-start.1
  27.5 0.0 all-reduce.3.cloned.1.call-start
  27.6 0.5 broadcast.7
  28.1 0.7 reduce.5
  28.8 0.1 reshape.30.req_ref
  28.8 23.4 %all-to-all-done.1 = f32[8,2,128,128]{3,2,1,0:T(8,128)S(1)} async-done(((f32[8,2,128,128]{3,2,1,0:T(8,128)}), f32[8,2,128,128]{3,2,1,0:T(8,128)S(1)}, u32[]{:S(2)}, u32[]{:S(2)}) %all-to-all-start.1) | async-done | bytes 1048608 | tf_op jit(solution)/shard_map/all_to_all | solution.py:238
  52.3 0.0 copy-done.1
  52.3 23.0 %sweep.2 = (f32[2,32,8,1024]{3,2,1,0:T(8,128)}, f32[9,128,128]{2,1,0:T(8,128)}) custom-call(s32[48]{0:T(128)S(1)} %reshape.30.req_ref, f32[2,32,8,1024]{3,2,1,0:T(8,128)} %bitcast.11, f32[4,2,128,128]{3,2,1,0:T(8,128)S(1)} %copy-done, bf16[4,256,256]{2,1,0:T(8,128)(2,1)S(1)} %copy-done.1, f32[16,128,128]{2,1,0:T(8,128)S(1)} %bitcast.7), custom_call_target="tpu_custom_call" | custom-call | tf_op jit(solution)/shard_map/sweep/pallas_call | solution.py:200
  75.3 0.0 all-reduce.3.cloned.1.call-update
  75.3 0.0 all-reduce.5.cloned.1.call-start
  75.3 138.1 %all-reduce.3.cloned.1.call-done = f32[9,128,128]{2,1,0:T(8,128)} async-done(((f32[9,128,128]{2,1,0:T(8,128)}), f32[9,128,128]{2,1,0:T(8,128)}) %all-reduce.3.cloned.1.call-update) | async-done | bytes 589840 | tf_op jit(solution)/shard_map/psum | solution.py:246
  213.5 1.5 slice_reduce_fusion.1
  215.6 1.1 slice_divide_fusion.1
  216.7 0.1 add.17.probe_ref
  216.8 23.1 %sweep.3 = (f32[2,32,8,1024]{3,2,1,0:T(8,128)}, f32[9,128,128]{2,1,0:T(8,128)}) custom-call(s32[48]{0:T(128)S(1)} %reshape.30.req_ref, f32[2,32,8,1024]{3,2,1,0:T(8,128)} %get-tuple-element.10.spec_ref, f32[4,2,128,128]{3,2,1,0:T(8,128)S(1)} %add.17.probe_ref, bf16[4,256,256]{2,1,0:T(8,128)(2,1)S(1)} %copy-done.1, f32[16,128,128]{2,1,0:T(8,128)S(1)} %bitcast.8), custom_call_target="tpu_custom_call" | custom-call | tf_op jit(solution)/shard_map/sweep/pallas_call | solution.py:200
  239.9 0.0 all-reduce.5.cloned.1.call-update
  239.9 140.3 %all-reduce.5.cloned.1.call-done = f32[9,128,128]{2,1,0:T(8,128)} async-done(((f32[9,128,128]{2,1,0:T(8,128)}), f32[9,128,128]{2,1,0:T(8,128)}) %all-reduce.5.cloned.1.call-update) | async-done | bytes 589840 | tf_op jit(solution)/shard_map/psum | solution.py:246
  380.2 1.5 slice_reduce_fusion
  382.3 1.1 slice_divide_fusion
  383.4 0.9 add.19
  (2 shorter events, 0.0 us)
Async XLA Ops:
  7.2 45.1 %copy-start.1 = (bf16[4,256,256]{2,1,0:T(8,128)(2,1)S(1)}, bf16[4,256,256]{2,1,0:T(8,128)(2,1)}, u32[]{:S(2)}) copy-start(bf16[4,256,256]{2,1,0:T(8,128)(2,1)} %constant.6.clone.table_ref) | copy-start | bytes 1572868
  7.2 45.1 %copy-start = (f32[4,2,128,128]{3,2,1,0:T(8,128)S(1)}, f32[4,2,128,128]{3,2,1,0:T(8,128)}, u32[]{:S(2)}) copy-start(f32[4,2,128,128]{3,2,1,0:T(8,128)} %probe_ref.1) | copy-start | bytes 1572868
  24.0 28.3 %all-to-all-start.1 = ((f32[8,2,128,128]{3,2,1,0:T(8,128)}), f32[8,2,128,128]{3,2,1,0:T(8,128)S(1)}, u32[]{:S(2)}, u32[]{:S(2)}) async-start(f32[8,2,128,128]{3,2,1,0:T(8,128)} %bitcast.12), calls=%async_computation.1 | async-start | bytes 2097152 | tf_op jit(solution)/shard_map/all_to_all | solution.py:238
  27.5 185.9 %all-reduce.3.cloned.1.call-start = ((), (), s32[]{:S(2)}) async-start(), calls=%async_computation.2 | async-start | bytes 1179648 | tf_op jit(solution)/shard_map/psum | solution.py:246
  75.3 304.9 %all-reduce.5.cloned.1.call-start = ((), (), s32[]{:S(2)}) async-start(), calls=%async_computation.3 | async-start | bytes 1179648 | tf_op jit(solution)/shard_map/psum | solution.py:246
Sparse Core Ops, SparseCore 0:
  75.4 138.0 all-reduce.2
  240.0 140.1 all-reduce.4

commit v2 on v1

--- a/solution.py
+++ b/solution.py
@@ -55,37 +55,186 @@
 
 
 def bucket_kernel(capacity, tile_ref, row_ref, col_ref, patterns_ref, grid_ref, req_ref):
-    own = patterns_ref.shape[0]
-
-    def clear(j, carry):
-        req_ref[j] = 0
-        return carry
-
-    lax.fori_loop(0, req_ref.shape[0], clear, 0)
+    own, window, _ = patterns_ref.shape
+    req_ref[...] = jnp.zeros_like(req_ref)
     for p in range(own):
         tile = tile_ref[p]
         rank = jnp.int32(0)
         for q in range(p):
             rank = rank + (tile_ref[q] == tile).astype(jnp.int32)
-        slot = tile * capacity + rank
-        grid_ref[slot] = patterns_ref[p]
-        req_ref[slot * 3] = row_ref[p]
-        req_ref[slot * 3 + 1] = col_ref[p]
-        req_ref[slot * 3 + 2] = jnp.int32(1)
-
-
-def bucket(tile_row, row_offset, col_offset, patterns, slots, capacity):
+        grid_ref[tile * capacity + rank] = patterns_ref[p]
+        for k, value in enumerate((row_ref[p], col_ref[p], jnp.int32(1))):
+            req_ref[tile, pl.ds(rank * 3 + k, 1), :] = jnp.full((1, window), value, jnp.int32)
+
+
+def bucket(tile_row, row_offset, col_offset, patterns, grid_rows, capacity):
     window = patterns.shape[-1]
+    head = -(-capacity * 3 // 8) * 8
     return pl.pallas_call(
         functools.partial(bucket_kernel, capacity),
         out_shape=(
-            jax.ShapeDtypeStruct((slots, window, window), jnp.float32),
-            jax.ShapeDtypeStruct((slots * 3,), jnp.int32),
+            jax.ShapeDtypeStruct((grid_rows * capacity, window, window), jnp.float32),
+            jax.ShapeDtypeStruct((grid_rows, head, window), jnp.int32),
         ),
         in_specs=[pl.BlockSpec(memory_space=SMEM)] * 3 + [pl.BlockSpec(memory_space=VMEM)],
-        out_specs=(pl.BlockSpec(memory_space=VMEM), pl.BlockSpec(memory_space=SMEM)),
+        out_specs=(pl.BlockSpec(memory_space=VMEM), pl.BlockSpec(memory_space=VMEM)),
         name="bucket",
     )(tile_row, row_offset, col_offset, patterns)
+
+
+def far_first(count):
+    return sorted(range(1, count), key=lambda d: -min(d, count - d))
+
+
+def exchange_kernel(count, grid_ref, req_ref, got_ref, seen_ref, own_sem, send_sem, recv_sem, hsend, hrecv):
+    me = lax.axis_index("ty")
+    barrier = pltpu.get_barrier_semaphore()
+    for d in range(1, count):
+        pl.semaphore_signal(
+            barrier, inc=1, device_id={"ty": lax.rem(me + d, count)}, device_id_type=pl.DeviceIdType.MESH
+        )
+    pl.semaphore_wait(barrier, count - 1)
+    copies = []
+    for d in range(1, count):
+        peer = lax.rem(me + d, count)
+        copies.append(pltpu.make_async_remote_copy(
+            src_ref=req_ref.at[peer], dst_ref=seen_ref.at[me],
+            send_sem=hsend.at[d - 1], recv_sem=hrecv.at[d - 1],
+            device_id={"ty": peer}, device_id_type=pl.DeviceIdType.MESH,
+        ))
+        copies[-1].start()
+    for d in far_first(count):
+        peer = lax.rem(me + d, count)
+        copies.append(pltpu.make_async_remote_copy(
+            src_ref=grid_ref.at[peer], dst_ref=got_ref.at[me],
+            send_sem=send_sem.at[d - 1], recv_sem=recv_sem.at[d - 1],
+            device_id={"ty": peer}, device_id_type=pl.DeviceIdType.MESH,
+        ))
+        copies[-1].start()
+    own = [
+        pltpu.make_async_copy(grid_ref.at[me], got_ref.at[me], own_sem.at[0]),
+        pltpu.make_async_copy(req_ref.at[me], seen_ref.at[me], own_sem.at[1]),
+    ]
+    for copy in own:
+        copy.start()
+    for copy in own + copies:
+        copy.wait()
+
+
+def exchange(grid, requests):
+    count = grid.shape[0]
+    dma = pltpu.SemaphoreType.DMA
+    return pl.pallas_call(
+        functools.partial(exchange_kernel, count),
+        out_shape=(
+            jax.ShapeDtypeStruct(grid.shape, grid.dtype),
+            jax.ShapeDtypeStruct(requests.shape, requests.dtype),
+        ),
+        in_specs=[pl.BlockSpec(memory_space=VMEM)] * 2,
+        out_specs=(pl.BlockSpec(memory_space=pl.ANY),) * 2,
+        scratch_shapes=[dma((2,))] + [dma((count - 1,))] * 4,
+        compiler_params=pltpu.CompilerParams(collective_id=0, has_side_effects=True),
+        name="exchange",
+    )(grid, requests)
+
+
+def total_kernel(ny, nty, g_ref, out_ref, half, part, piece, in_y, in_ty, full, *sems):
+    core_s, core_r, y_s, y_r, ty_s, ty_r, ty_s2, ty_r2, y_s2, y_r2, core_s2, core_r2 = sems
+    ty, tx = lax.axis_index("ty"), lax.axis_index("tx")
+    core, y = lax.rem(tx, 2), tx // 2
+    mate = {"tx": y * 2 + 1 - core}
+    y_ids = [lax.rem(y + d, ny) for d in range(1, ny)]
+    ty_ids = [lax.rem(ty + d, nty) for d in range(1, nty)]
+    y_dev = [{"tx": peer * 2 + core} for peer in y_ids]
+    ty_dev = [{"ty": peer} for peer in ty_ids]
+    mesh_id = pl.DeviceIdType.MESH
+    barrier = pltpu.get_barrier_semaphore()
+    for device in [mate] + y_dev + ty_dev:
+        pl.semaphore_signal(barrier, inc=1, device_id=device, device_id_type=mesh_id)
+    pl.semaphore_wait(barrier, 1 + len(y_dev) + len(ty_dev))
+
+    def send(src, dst, s, r, device):
+        copy = pltpu.make_async_remote_copy(
+            src_ref=src, dst_ref=dst, send_sem=s, recv_sem=r, device_id=device, device_id_type=mesh_id
+        )
+        copy.start()
+        return copy
+
+    send(g_ref.at[1 - core], half, core_s.at[0], core_r.at[0], mate).wait()
+    part[...] = g_ref[core] + half[...]
+    copies = [
+        send(part.at[y_ids[d]], in_y.at[d], y_s.at[d], y_r.at[d], y_dev[d]) for d in range(ny - 1)
+    ]
+    acc = part[y]
+    for d, copy in enumerate(copies):
+        copy.wait()
+        acc = acc + in_y[d]
+    piece[...] = acc
+    order = [d - 1 for d in far_first(nty)]
+    copies = {
+        d: send(piece.at[ty_ids[d]], in_ty.at[d], ty_s.at[d], ty_r.at[d], ty_dev[d]) for d in order
+    }
+    acc = piece[ty]
+    for d in range(nty - 1):
+        copies[d].wait()
+        acc = acc + in_ty[d]
+    full[core, y, ty] = acc
+    mine = full.at[core, y, ty]
+    copies = [send(mine, mine, ty_s2.at[d], ty_r2.at[d], ty_dev[d]) for d in order]
+    for copy in copies:
+        copy.wait()
+    mine = full.at[core, y]
+    copies = [send(mine, mine, y_s2.at[d], y_r2.at[d], y_dev[d]) for d in range(ny - 1)]
+    for copy in copies:
+        copy.wait()
+    mine = full.at[core]
+    send(mine, mine, core_s2.at[0], core_r2.at[0], mate).wait()
+    out_ref[...] = full[...]
+
+
+def total_over_devices(grads):
+    window = grads.shape[-1]
+    nty, ny = lax.axis_size("ty"), lax.axis_size("tx") // 2
+    c = grads.size // (2 * ny * nty * 8 * window)
+    shape = (2, ny, nty, c, 8, window)
+    f32 = jnp.float32
+    dma = pltpu.SemaphoreType.DMA
+    y_n, ty_n = max(ny - 1, 1), max(nty - 1, 1)
+    total = pl.pallas_call(
+        functools.partial(total_kernel, ny, nty),
+        out_shape=jax.ShapeDtypeStruct(shape, f32),
+        in_specs=[pl.BlockSpec(memory_space=VMEM)],
+        out_specs=pl.BlockSpec(memory_space=VMEM),
+        scratch_shapes=[
+            VMEM(shape[1:], f32),
+            VMEM(shape[1:], f32),
+            VMEM(shape[2:], f32),
+            VMEM((y_n,) + shape[2:], f32),
+            VMEM((ty_n,) + shape[3:], f32),
+            VMEM(shape, f32),
+        ] + [dma((n,)) for n in (1, 1, y_n, y_n, ty_n, ty_n, ty_n, ty_n, y_n, y_n, 1, 1)],
+        compiler_params=pltpu.CompilerParams(collective_id=1, has_side_effects=True),
+        name="total",
+    )(grads.reshape(shape))
+    return total.reshape(grads.shape)
+
+
+def update_kernel(total_ref, probe_ref, out_ref):
+    planes = probe_ref.shape[0]
+    bottom = jnp.max(total_ref[planes]) + SMALL_EPS
+    out_ref[...] = probe_ref[...] + total_ref[:planes] / bottom
+
+
+def update(total, probe_modes):
+    modes, _, window, _ = probe_modes.shape
+    shape = (2 * modes, window, window)
+    return pl.pallas_call(
+        update_kernel,
+        out_shape=jax.ShapeDtypeStruct(shape, jnp.float32),
+        in_specs=[pl.BlockSpec(memory_space=VMEM)] * 2,
+        out_specs=pl.BlockSpec(memory_space=VMEM),
+        name="update",
+    )(total, probe_modes.reshape(shape)).reshape(probe_modes.shape)
 
 
 def sweep_kernel(req_ref, spec_ref, probe_ref, table_ref, pattern_ref, out_ref, grad_ref, scale_ref, far_ref):
@@ -193,7 +342,7 @@
             )
 
 
-def sweep(requests, specimen, probe_modes, tables, measured):
+def sweep(requests, specimen, probe_modes, tables, measured, blocks):
     slots, window, _ = measured.shape
     modes = probe_modes.shape[0]
     whole = lambda shape: pl.BlockSpec(shape, lambda i: (0,) * len(shape))
@@ -202,7 +351,7 @@
         grid=(slots,),
         out_shape=(
             jax.ShapeDtypeStruct(specimen.shape, jnp.float32),
-            jax.ShapeDtypeStruct((2 * modes + 1, window, window), jnp.float32),
+            jax.ShapeDtypeStruct((blocks, window, window), jnp.float32),
         ),
         in_specs=[
             pl.BlockSpec(memory_space=SMEM),
@@ -211,7 +360,7 @@
             whole(tables.shape),
             pl.BlockSpec((1, window, window), lambda i: (i, 0, 0)),
         ],
-        out_specs=(whole(specimen.shape), whole((2 * modes + 1, window, window))),
+        out_specs=(whole(specimen.shape), whole((blocks, window, window))),
         scratch_shapes=[
             pltpu.SMEM((1,), jnp.float32),
             pltpu.VMEM((modes, window, 2 * window), jnp.float32),
@@ -231,22 +380,21 @@
     capacity = max(2, 2 * own_count // grid_rows)
     slots = grid_rows * capacity
     tables = jnp.asarray(dft_tables(window))
-    pattern_grid, requests = bucket(tile_row, row_offset, col_offset, patterns, slots, capacity)
-    seen = lax.all_to_all(
-        requests.reshape(grid_rows, capacity * 3), "ty", split_axis=0, concat_axis=0, tiled=True
-    ).reshape(slots * 3)
-    measured = lax.all_to_all(
-        pattern_grid.reshape(grid_rows, capacity, window, window),
-        "ty", split_axis=0, concat_axis=0, tiled=True,
-    ).reshape(slots, window, window)
+    pattern_grid, requests = bucket(tile_row, row_offset, col_offset, patterns, grid_rows, capacity)
+    measured, seen = exchange(
+        pattern_grid.reshape(grid_rows, capacity, window, window), requests
+    )
+    measured = measured.reshape(slots, window, window)
+    seen = seen[:, : capacity * 3, 0].reshape(slots * 3)
+    devices = grid_rows * lax.axis_size("tx")
+    tiles = window // 8
+    per_device = -(-(2 * modes + 1) * tiles // devices)
+    blocks = -(-per_device * devices // tiles)
     shape = specimen.shape
     specimen = specimen.reshape(2, shape[1] // 8, 8, shape[2])
     for sweep_index in range(ITERS):
-        specimen, grads = sweep(seen, specimen, probe_modes, tables, measured)
-        total = lax.psum(grads, ("ty", "tx"))
-        probe_modes = probe_modes + total[: 2 * modes].reshape(probe_modes.shape) / (
-            jnp.max(total[2 * modes]) + SMALL_EPS
-        )
+        specimen, grads = sweep(seen, specimen, probe_modes, tables, measured, blocks)
+        probe_modes = update(total_over_devices(grads), probe_modes)
     return (specimen.reshape(shape), probe_modes)
 
 

time: 392 us -> 171 us (0.44)
  waiting for transfers between devices: 302 us -> 0 us
  Pallas kernels: 48.6 us -> 161 us
  between operations: 15.4 us -> 0.67 us
  blocking collectives: 13.6 us -> 0 us
  other arithmetic: 6.7 us -> 0 us
  local copies, waits for them, and re-layouts: 1.34 us -> 7.09 us
    psum x2 -> x0, waiting for transfers between devices: 278 us -> none  [shards(): total = lax.psum(grads, ('ty', 'tx'))]
    pallas_call x0 -> x5, Pallas kernels: none -> 109 us  [the longest x2 78.7 us: total_over_devices(): pl.pallas_call(functools.partial(total_kernel, ny, nty), out_shape=jax.Sh...]
    all_to_all x1 -> x0, waiting for transfers between devices: 23.4 us -> none  [shards(): lax.all_to_all(pattern_grid.reshape(grid_rows, capacity, window, window),...]
    all_to_all x1 -> x0, blocking collectives: 13.6 us -> none  [shards(): lax.all_to_all(requests.reshape(grid_rows, capacity * 3), 'ty', split_axi...]
    unnamed x4 -> x16, local copies, waits for them, and re-layouts: 0.01 us -> 6.05 us
  transfers between devices with their start and end apart: 3 -> 0, of which waited for: 3 -> 0; matrix products, arithmetic and copies ran while one was open for 0% -> 0% of each run, Pallas kernels for 0% -> 0%
where the time goes in v2:
time: 171 us; the launch traced here: 169 us
  Pallas kernels  161 us (94%)
  local copies, waits for them, and re-layouts  7.09 us (4%)
    pallas_call x2, Pallas kernels, total_over_devices(): pl.pallas_call(functools.partial(total_kernel, ny, nty), out_shape=jax.Sh...  78.7 us
    pallas_call x2, Pallas kernels, sweep(): pl.pallas_call(sweep_kernel, grid=(slots,), out_shape=(jax.ShapeDtypeStru...  50 us
    pallas_call x1, Pallas kernels, exchange(): pl.pallas_call(functools.partial(exchange_kernel, count), out_shape=(jax....  26.2 us
    unnamed x16, local copies, waits for them, and re-layouts  6.05 us
    pallas_call x2, Pallas kernels, update(): pl.pallas_call(update_kernel, out_shape=jax.ShapeDtypeStruct(shape, jnp.f...  4.48 us

profile of v2, /device:TPU:0, one launch (start us, length us, event | category | flops | bytes accessed | tf_op | source)
XLA Modules:
  0.0 169.2 jit_solution(10017576861244270116)
XLA Ops:
  0.6 2.1 %bucket.1 = (f32[16,128,128]{2,1,0:T(8,128)}, s32[8,8,128]{2,1,0:T(8,128)}) custom-call(s32[8]{0:T(128)} %tile_ref.1, s32[8]{0:T(128)} %row_ref.1, s32[8]{0:T(128)} %col_ref.1, f32[8,128,128]{2,1,0:T(8,128)} %patterns_ref.1), custom_call_target="tpu_custom_call" | custom-call | tf_op jit(solution)/shard_map/bucket/pallas_call | solution.py:73
  2.7 26.2 %exchange.1 = (f32[8,2,128,128]{3,2,1,0:T(8,128)}, s32[8,8,128]{2,1,0:T(8,128)}) custom-call(f32[8,2,128,128]{3,2,1,0:T(8,128)} %bitcast.20, s32[8,8,128]{2,1,0:T(8,128)} %get-tuple-element.11.req_ref), custom_call_target="tpu_custom_call" | custom-call | tf_op jit(solution)/shard_map/exchange/pallas_call | solution.py:127
  28.9 1.0 slice_reduce_fusion
  29.9 0.1 reshape_squeeze.3.req_ref
  30.0 0.0 copy-start.1
  30.0 1.2 copy-done.1
  31.2 0.0 copy-start.3
  31.2 1.0 copy-done.3
  32.3 0.0 copy-start.5
  32.3 1.0 copy-done.5
  33.3 25.2 %sweep.2 = (f32[2,32,8,1024]{3,2,1,0:T(8,128)}, f32[10,128,128]{2,1,0:T(8,128)S(1)}) custom-call(s32[48]{0:T(128)S(1)} %reshape_squeeze.3.req_ref, f32[2,32,8,1024]{3,2,1,0:T(8,128)} %bitcast.19, f32[4,2,128,128]{3,2,1,0:T(8,128)S(1)} %copy-done.5, bf16[4,256,256]{2,1,0:T(8,128)(2,1)S(1)} %copy-done.3, f32[16,128,128]{2,1,0:T(8,128)S(1)} %bitcast.12), custom_call_target="tpu_custom_call" | custom-call | tf_op jit(solution)/shard_map/sweep/pallas_call | solution.py:349
  58.5 0.0 copy-start.7
  58.5 0.8 copy-done.7
  59.4 0.0 copy-start.2
  59.4 0.0 copy-start.4
  59.4 41.7 %total.2 = f32[2,2,8,5,8,128]{5,4,3,2,1,0:T(8,128)} custom-call(f32[2,2,8,5,8,128]{5,4,3,2,1,0:T(8,128)} %bitcast.16), custom_call_target="tpu_custom_call" | custom-call | tf_op jit(solution)/shard_map/total/pallas_call | solution.py:203
  101.1 2.2 %update.2.probe_ref = f32[8,128,128]{2,1,0:T(8,128)} custom-call(f32[10,128,128]{2,1,0:T(8,128)} %bitcast.18, f32[8,128,128]{2,1,0:T(8,128)} %bitcast.14), custom_call_target="tpu_custom_call" | custom-call | tf_op jit(solution)/shard_map/update/pallas_call | solution.py:231
  103.4 0.0 copy-done.2
  103.4 0.0 copy-done.4
  103.4 1.0 copy-done
  104.4 24.7 %sweep.3 = (f32[2,32,8,1024]{3,2,1,0:T(8,128)}, f32[10,128,128]{2,1,0:T(8,128)S(1)}) custom-call(s32[48]{0:T(128)S(1)} %reshape_squeeze.3.req_ref, f32[2,32,8,1024]{3,2,1,0:T(8,128)} %get-tuple-element.14.spec_ref, f32[4,2,128,128]{3,2,1,0:T(8,128)S(1)} %bitcast.11, bf16[4,256,256]{2,1,0:T(8,128)(2,1)S(1)} %copy-done.4, f32[16,128,128]{2,1,0:T(8,128)S(1)} %bitcast.13), custom_call_target="tpu_custom_call" | custom-call | tf_op jit(solution)/shard_map/sweep/pallas_call | solution.py:349
  129.1 0.8 copy-done.6
  130.0 36.9 %total.3 = f32[2,2,8,5,8,128]{5,4,3,2,1,0:T(8,128)} custom-call(f32[2,2,8,5,8,128]{5,4,3,2,1,0:T(8,128)} %bitcast.15), custom_call_target="tpu_custom_call" | custom-call | tf_op jit(solution)/shard_map/total/pallas_call | solution.py:203
  166.9 2.2 %update.3 = f32[8,128,128]{2,1,0:T(8,128)} custom-call(f32[10,128,128]{2,1,0:T(8,128)} %bitcast.17, f32[8,128,128]{2,1,0:T(8,128)} %update.2.probe_ref), custom_call_target="tpu_custom_call" | custom-call | tf_op jit(solution)/shard_map/update/pallas_call | solution.py:231
  (2 shorter events, 0.0 us)
Async XLA Ops:
  30.0 1.2 copy-start.1
  31.2 1.0 copy-start.3
  32.3 1.0 copy-start.5
  58.5 0.8 copy-start.7
  59.4 44.0 %copy-start.2 = (f32[8,2,128,128]{3,2,1,0:T(8,128)S(1)}, f32[8,2,128,128]{3,2,1,0:T(8,128)}, u32[]{:S(2)}) copy-start(f32[8,2,128,128]{3,2,1,0:T(8,128)} %get-tuple-element.13) | copy-start | bytes 3145732
  59.4 44.0 %copy-start.4 = (bf16[4,256,256]{2,1,0:T(8,128)(2,1)S(1)}, bf16[4,256,256]{2,1,0:T(8,128)(2,1)}, u32[]{:S(2)}) copy-start(bf16[4,256,256]{2,1,0:T(8,128)(2,1)} %constant.2.clone.table_ref) | copy-start | bytes 1572868
  103.4 1.0 copy-start
  129.1 0.8 copy-start.6

commit v3 on v2

--- a/solution.py
+++ b/solution.py
@@ -160,11 +160,16 @@
         copy.start()
         return copy
 
-    send(g_ref.at[1 - core], half, core_s.at[0], core_r.at[0], mate).wait()
-    part[...] = g_ref[core] + half[...]
-    copies = [
-        send(part.at[y_ids[d]], in_y.at[d], y_s.at[d], y_r.at[d], y_dev[d]) for d in range(ny - 1)
+    halves = [
+        send(g_ref.at[1 - core, k], half.at[k], core_s.at[d], core_r.at[d], mate)
+        for d, k in enumerate(y_ids + [y])
     ]
+    copies = []
+    for d, k in enumerate(y_ids + [y]):
+        halves[d].wait()
+        part[k] = g_ref[core, k] + half[k]
+        if d < ny - 1:
+            copies.append(send(part.at[k], in_y.at[d], y_s.at[d], y_r.at[d], y_dev[d]))
     acc = part[y]
     for d, copy in enumerate(copies):
         copy.wait()
@@ -185,10 +190,13 @@
         copy.wait()
     mine = full.at[core, y]
     copies = [send(mine, mine, y_s2.at[d], y_r2.at[d], y_dev[d]) for d in range(ny - 1)]
-    for copy in copies:
+    last = [send(mine, mine, core_s2.at[ny - 1], core_r2.at[ny - 1], mate)]
+    for d, copy in enumerate(copies):
         copy.wait()
-    mine = full.at[core]
-    send(mine, mine, core_s2.at[0], core_r2.at[0], mate).wait()
+        other = full.at[core, lax.rem(y + ny - 1 - d, ny)]
+        last.append(send(other, other, core_s2.at[d], core_r2.at[d], mate))
+    for copy in last:
+        copy.wait()
     out_ref[...] = full[...]
 
 
@@ -212,7 +220,7 @@
             VMEM((y_n,) + shape[2:], f32),
             VMEM((ty_n,) + shape[3:], f32),
             VMEM(shape, f32),
-        ] + [dma((n,)) for n in (1, 1, y_n, y_n, ty_n, ty_n, ty_n, ty_n, y_n, y_n, 1, 1)],
+        ] + [dma((n,)) for n in (ny, ny, y_n, y_n, ty_n, ty_n, ty_n, ty_n, y_n, y_n, ny, ny)],
         compiler_params=pltpu.CompilerParams(collective_id=1, has_side_effects=True),
         name="total",
     )(grads.reshape(shape))

time: 171 us -> 170 us (level)
    pallas_call x2, Pallas kernels: 78.7 us -> 102 us  [total_over_devices(): pl.pallas_call(functools.partial(total_kernel, ny, nty), out_shape=jax.Sh...]
    pallas_call x2, Pallas kernels: 50 us -> 26.9 us  [sweep(): pl.pallas_call(sweep_kernel, grid=(slots,), out_shape=(jax.ShapeDtypeStru...]
where the time goes in v3:
time: 170 us; the launch traced here: 169 us
  Pallas kernels  161 us (95%)
  local copies, waits for them, and re-layouts  7.09 us (4%)
    pallas_call x2, Pallas kernels, total_over_devices(): pl.pallas_call(functools.partial(total_kernel, ny, nty), out_shape=jax.Sh...  102 us
    pallas_call x2, Pallas kernels, sweep(): pl.pallas_call(sweep_kernel, grid=(slots,), out_shape=(jax.ShapeDtypeStru...  26.9 us
    pallas_call x1, Pallas kernels, exchange(): pl.pallas_call(functools.partial(exchange_kernel, count), out_shape=(jax....  26.2 us
    unnamed x16, local copies, waits for them, and re-layouts  6.05 us
    pallas_call x2, Pallas kernels, update(): pl.pallas_call(update_kernel, out_shape=jax.ShapeDtypeStruct(shape, jnp.f...  4.48 us

profile of v3, /device:TPU:0, one launch (start us, length us, event | category | flops | bytes accessed | tf_op | source)
XLA Modules:
  0.0 169.2 jit_solution(17068182557158419383)
XLA Ops:
  0.6 2.1 %bucket.1 = (f32[16,128,128]{2,1,0:T(8,128)}, s32[8,8,128]{2,1,0:T(8,128)}) custom-call(s32[8]{0:T(128)} %tile_ref.1, s32[8]{0:T(128)} %row_ref.1, s32[8]{0:T(128)} %col_ref.1, f32[8,128,128]{2,1,0:T(8,128)} %patterns_ref.1), custom_call_target="tpu_custom_call" | custom-call | tf_op jit(solution)/shard_map/bucket/pallas_call | solution.py:73
  2.7 26.2 %exchange.1 = (f32[8,2,128,128]{3,2,1,0:T(8,128)}, s32[8,8,128]{2,1,0:T(8,128)}) custom-call(f32[8,2,128,128]{3,2,1,0:T(8,128)} %bitcast.20, s32[8,8,128]{2,1,0:T(8,128)} %get-tuple-element.11.req_ref), custom_call_target="tpu_custom_call" | custom-call | tf_op jit(solution)/shard_map/exchange/pallas_call | solution.py:127
  28.9 1.0 slice_reduce_fusion
  29.9 0.1 reshape_squeeze.3.req_ref
  30.0 0.0 copy-start.1
  30.0 1.2 copy-done.1
  31.2 0.0 copy-start.3
  31.2 1.0 copy-done.3
  32.3 0.0 copy-start.5
  32.3 1.0 copy-done.5
  33.3 13.6 %sweep.2 = (f32[2,32,8,1024]{3,2,1,0:T(8,128)}, f32[10,128,128]{2,1,0:T(8,128)S(1)}) custom-call(s32[48]{0:T(128)S(1)} %reshape_squeeze.3.req_ref, f32[2,32,8,1024]{3,2,1,0:T(8,128)} %bitcast.19, f32[4,2,128,128]{3,2,1,0:T(8,128)S(1)} %copy-done.5, bf16[4,256,256]{2,1,0:T(8,128)(2,1)S(1)} %copy-done.3, f32[16,128,128]{2,1,0:T(8,128)S(1)} %bitcast.12), custom_call_target="tpu_custom_call" | custom-call | tf_op jit(solution)/shard_map/sweep/pallas_call | solution.py:357
  46.9 0.0 copy-start.7
  46.9 0.8 copy-done.7
  47.7 0.0 copy-start.2
  47.7 0.0 copy-start.4
  47.7 53.9 %total.2 = f32[2,2,8,5,8,128]{5,4,3,2,1,0:T(8,128)} custom-call(f32[2,2,8,5,8,128]{5,4,3,2,1,0:T(8,128)} %bitcast.16), custom_call_target="tpu_custom_call" | custom-call | tf_op jit(solution)/shard_map/total/pallas_call | solution.py:211
  101.6 2.2 %update.2.probe_ref = f32[8,128,128]{2,1,0:T(8,128)} custom-call(f32[10,128,128]{2,1,0:T(8,128)} %bitcast.18, f32[8,128,128]{2,1,0:T(8,128)} %bitcast.14), custom_call_target="tpu_custom_call" | custom-call | tf_op jit(solution)/shard_map/update/pallas_call | solution.py:239
  103.9 0.0 copy-done.2
  103.9 0.0 copy-done.4
  103.9 1.0 copy-done
  104.9 13.3 %sweep.3 = (f32[2,32,8,1024]{3,2,1,0:T(8,128)}, f32[10,128,128]{2,1,0:T(8,128)S(1)}) custom-call(s32[48]{0:T(128)S(1)} %reshape_squeeze.3.req_ref, f32[2,32,8,1024]{3,2,1,0:T(8,128)} %get-tuple-element.14.spec_ref, f32[4,2,128,128]{3,2,1,0:T(8,128)S(1)} %bitcast.11, bf16[4,256,256]{2,1,0:T(8,128)(2,1)S(1)} %copy-done.4, f32[16,128,128]{2,1,0:T(8,128)S(1)} %bitcast.13), custom_call_target="tpu_custom_call" | custom-call | tf_op jit(solution)/shard_map/sweep/pallas_call | solution.py:357
  118.2 0.8 copy-done.6
  119.1 47.9 %total.3 = f32[2,2,8,5,8,128]{5,4,3,2,1,0:T(8,128)} custom-call(f32[2,2,8,5,8,128]{5,4,3,2,1,0:T(8,128)} %bitcast.15), custom_call_target="tpu_custom_call" | custom-call | tf_op jit(solution)/shard_map/total/pallas_call | solution.py:211
  167.0 2.2 %update.3 = f32[8,128,128]{2,1,0:T(8,128)} custom-call(f32[10,128,128]{2,1,0:T(8,128)} %bitcast.17, f32[8,128,128]{2,1,0:T(8,128)} %update.2.probe_ref), custom_call_target="tpu_custom_call" | custom-call | tf_op jit(solution)/shard_map/update/pallas_call | solution.py:239
  (2 shorter events, 0.0 us)
Async XLA Ops:
  30.0 1.2 copy-start.1
  31.2 1.0 copy-start.3
  32.3 1.0 copy-start.5
  46.9 0.8 copy-start.7
  47.7 56.1 %copy-start.2 = (f32[8,2,128,128]{3,2,1,0:T(8,128)S(1)}, f32[8,2,128,128]{3,2,1,0:T(8,128)}, u32[]{:S(2)}) copy-start(f32[8,2,128,128]{3,2,1,0:T(8,128)} %get-tuple-element.13) | copy-start | bytes 3145732
  47.7 56.1 %copy-start.4 = (bf16[4,256,256]{2,1,0:T(8,128)(2,1)S(1)}, bf16[4,256,256]{2,1,0:T(8,128)(2,1)}, u32[]{:S(2)}) copy-start(bf16[4,256,256]{2,1,0:T(8,128)(2,1)} %constant.2.clone.table_ref) | copy-start | bytes 1572868
  103.9 1.0 copy-start
  118.2 0.8 copy-start.6
